TPU v7x, 256 devices: a whole 4x4x8 slice. The times are simulated.
256 devices in a mesh: tile: 64 (over z, y_lo, x), mode: 4 (over y_hi, core).
Axes of the slice: x: 4, y: 4 (y_hi: 2, y_lo: 2; y = y_hi * 2 + y_lo), z: 8, core: 2. Of those that a mesh axis runs over, the one named last changes fastest.
Arguments:
- object_tiles: float32 [64, 2, 2, 256, 256], P('tile'), may hold values from -6 to 6
- object_previous: float32 [64, 2, 2, 256, 256], P('tile'), may hold values from -6 to 6
- probe: float32 [4, 8, 2, 256, 256], P(None, 'mode', None, 'tile'), may hold values from -2 to 2
- probe_previous: float32 [4, 8, 2, 256, 256], P(None, 'mode', None, 'tile'), may hold values from -6 to 6
- patterns: float32 [128, 256, 256], P('tile'), may hold values from 0 to 2
- offsets: int32 [2, 128], P(None, 'tile'), may hold values from 0 to 255
- scan_of_slot: int32 [128], P('tile'), may hold values from 0 to 3
- tile_load: int32 [64], P('tile'), may hold values from 1 to 2, as said below
- step_sizes: int32 [2], replicated, may hold values from 128 to 511
- object_norm_before: float32 [1], replicated, may hold values from 0.1 to 0.4
- probe_norm_before: float32 [1], replicated, may hold values from 12 to 64
Outputs:
- new_object: float32 [64, 2, 2, 256, 256], P('tile')
- object_direction: float32 [64, 2, 2, 256, 256], P('tile')
- new_probe: float32 [4, 8, 2, 256, 256], P(None, 'mode', None, 'tile')
- probe_direction: float32 [4, 8, 2, 256, 256], P(None, 'mode', None, 'tile')
Inputs may be any that keep to these rules, and one draw needn't show every extreme that they name: `tile_load`: every tile holds 1 to 2 used slots, and some tile holds exactly 2.
All inputs are finite; a program needn't handle non-finite values.
Results may differ from a plain program's by a relative error of at most 0.024.
Values may be sent and summed in bfloat16 or wider, within the bound.
No kernel may reach another device: no remote copies, remote signals or barrier semaphores. Data moves between devices by JAX's collectives and lax.ppermute only.
A program may use at most 64 MiB of HBM per device.

v0:
```python
import math
import jax
import jax.numpy as jnp
from jax import lax
from jax.sharding import PartitionSpec as P

TGX = 8
MODES = 8
SCAN_COUNT = 4
residual_weight = 2.0


def from_behind(block, axis, distance):
    devices = range(lax.axis_size(axis))
    route = [(i - distance, i) for i in devices if i - distance in devices]
    return lax.ppermute(block, axis, route)


def table_pair(width):
    index_row = jnp.arange(width, dtype=jnp.int32)
    product = index_row[:, None] * index_row[None, :] % width
    angle = product.astype(jnp.float32) * (2.0 * math.pi / width)
    factor = 1.0 / math.sqrt(width)
    cosine = (jnp.cos(angle) * factor).astype(jnp.bfloat16)
    sine = (-jnp.sin(angle) * factor).astype(jnp.bfloat16)
    index_free = jnp.where(index_row < width // 2, index_row, index_row - width).astype(jnp.float32)
    phase = (
        index_free[:, None] * index_free[:, None] + index_free[None, :] * index_free[None, :]
    ) * (math.pi / (4.0 * width))
    return (cosine, sine, jnp.cos(phase), jnp.sin(phase))


def right_product(left_data, table):
    return jnp.einsum("...jk,kl->...jl", left_data, table, preferred_element_type=jnp.float32)


def left_product(table, right_data):
    return jnp.einsum("ij,...jl->...il", table, right_data, preferred_element_type=jnp.float32)


def transform(wave_re, wave_im, tables, inverse):
    cosine = tables[0]
    sine = -tables[1] if inverse else tables[1]
    first_re = (right_product(wave_re, cosine) - right_product(wave_im, sine)).astype(jnp.bfloat16)
    first_im = (right_product(wave_re, sine) + right_product(wave_im, cosine)).astype(jnp.bfloat16)
    out_re = (left_product(cosine, first_re) - left_product(sine, first_im)).astype(jnp.bfloat16)
    out_im = (left_product(sine, first_re) + left_product(cosine, first_im)).astype(jnp.bfloat16)
    return (out_re, out_im)


def complex_times(first_re, first_im, second_re, second_im):
    first_portion = first_re.astype(jnp.float32)
    b_part = first_im.astype(jnp.float32)
    c_part = second_re.astype(jnp.float32)
    d_part = second_im.astype(jnp.float32)
    return (first_portion * c_part - b_part * d_part, first_portion * d_part + b_part * c_part)


def conj_times(first_re, first_im, second_re, second_im):
    first_portion = first_re.astype(jnp.float32)
    b_part = first_im.astype(jnp.float32)
    c_part = second_re.astype(jnp.float32)
    d_part = second_im.astype(jnp.float32)
    return (first_portion * c_part + b_part * d_part, first_portion * d_part - b_part * c_part)


def propagate(wave_re, wave_im, tables, adjoint):
    spec_re, spec_im = transform(wave_re, wave_im, tables, False)
    kernel_im = -tables[3] if adjoint else tables[3]
    moved_re, moved_im = complex_times(spec_re, spec_im, tables[2], kernel_im)
    return transform(moved_re.astype(jnp.bfloat16), moved_im.astype(jnp.bfloat16), tables, True)


def body(
    object_tiles,
    object_previous,
    probe,
    probe_previous,
    patterns,
    offsets,
    scan_of_slot,
    tile_load,
    step_sizes,
    object_norm_before,
    probe_norm_before,
):
    tile_count = lax.axis_size("tile")
    mode_count = lax.axis_size("mode")
    slots = patterns.shape[0]
    width = patterns.shape[1]
    layers = object_tiles.shape[1]
    tile_side = object_tiles.shape[3]
    scans = probe.shape[0]
    tables = table_pair(width)
    own_tile = object_tiles[0].astype(jnp.bfloat16)
    east_part = from_behind(own_tile, "tile", -1)
    upper = jnp.concatenate([own_tile, east_part], axis=3)
    lower = from_behind(upper, "tile", -TGX)
    region = jnp.concatenate([upper, lower], axis=2)
    gathered = lax.all_gather(probe.astype(jnp.bfloat16), "tile", axis=3, tiled=True)
    valid_mask = (jnp.arange(slots, dtype=jnp.int32) < tile_load[0]).astype(jnp.float32)

    def cut_patch(row_start, col_start):
        return lax.dynamic_slice(region, (0, 0, row_start, col_start), (layers, 2, width, width))

    patches = jax.vmap(cut_patch)(offsets[0], offsets[1])
    probe_pick = jnp.take(gathered, scan_of_slot, axis=0)
    wave_re = probe_pick[:, :, 0]
    wave_im = probe_pick[:, :, 1]
    incident = []
    for layer_index in range(layers):
        incident.append((wave_re, wave_im))
        next_re, next_im = complex_times(
            wave_re, wave_im, patches[:, None, layer_index, 0], patches[:, None, layer_index, 1]
        )
        wave_re = next_re.astype(jnp.bfloat16)
        wave_im = next_im.astype(jnp.bfloat16)
        if layer_index + 1 < layers:
            wave_re, wave_im = propagate(wave_re, wave_im, tables, False)
    far_re, far_im = transform(wave_re, wave_im, tables, False)
    far_re32 = far_re.astype(jnp.float32)
    far_im32 = far_im.astype(jnp.float32)
    partial_power = jnp.sum(far_re32 * far_re32 + far_im32 * far_im32, axis=1)
    power = lax.psum(partial_power, "mode")
    misfit = (power - patterns) * valid_mask[:, None, None]
    back_re = (residual_weight * misfit[:, None] * far_re32).astype(jnp.bfloat16)
    back_im = (residual_weight * misfit[:, None] * far_im32).astype(jnp.bfloat16)
    back_re, back_im = transform(back_re, back_im, tables, True)
    slice_terms = [None] * layers
    probe_terms = None
    for layer_index in reversed(range(layers)):
        inc_re, inc_im = incident[layer_index]
        grad_re, grad_im = conj_times(inc_re, inc_im, back_re, back_im)
        slice_terms[layer_index] = jnp.stack(
            [jnp.sum(grad_re, axis=1), jnp.sum(grad_im, axis=1)], axis=1
        )
        carry_re, carry_im = conj_times(
            patches[:, None, layer_index, 0], patches[:, None, layer_index, 1], back_re, back_im
        )
        if layer_index > 0:
            back_re, back_im = propagate(
                carry_re.astype(jnp.bfloat16), carry_im.astype(jnp.bfloat16), tables, True
            )
        else:
            probe_terms = jnp.stack([carry_re, carry_im], axis=2)
    slot_grads = jnp.stack(slice_terms, axis=1)
    region_grad = jnp.zeros((layers, 2, 2 * tile_side, 2 * tile_side), jnp.float32)
    for slot_index in range(slots):
        starts = (0, 0, offsets[0, slot_index], offsets[1, slot_index])
        current = lax.dynamic_slice(region_grad, starts, (layers, 2, width, width))
        region_grad = lax.dynamic_update_slice(
            region_grad, current + slot_grads[slot_index], starts
        )
    region_grad = lax.psum(region_grad.astype(jnp.bfloat16), "mode").astype(jnp.float32)
    from_above = from_behind(
        region_grad[:, :, tile_side:, :].astype(jnp.bfloat16), "tile", TGX
    ).astype(jnp.float32)
    upper_grad = region_grad[:, :, :tile_side, :] + from_above
    from_left = from_behind(upper_grad[:, :, :, tile_side:].astype(jnp.bfloat16), "tile", 1).astype(
        jnp.float32
    )
    tile_grad = upper_grad[:, :, :, :tile_side] + from_left
    scan_onehot = (scan_of_slot[:, None] == jnp.arange(scans, dtype=jnp.int32)[None, :]).astype(
        jnp.float32
    )
    probe_local = jnp.einsum(
        "cs,cmrij->smrij", scan_onehot, probe_terms, precision=lax.Precision.HIGHEST
    )
    probe_grad = lax.psum_scatter(probe_local, "tile", scatter_dimension=3, tiled=True)
    object_sum = jnp.sum(tile_grad * tile_grad) / float(mode_count)
    probe_sum = jnp.sum(probe_grad * probe_grad)
    object_total, probe_total = lax.psum((object_sum, probe_sum), ("tile", "mode"))
    object_square = object_total / float(tile_count * layers * 2 * tile_side * tile_side)
    probe_square = probe_total / float(SCAN_COUNT * MODES * 2 * width * width)
    object_direction = -tile_grad[None] + object_square / object_norm_before[0] * object_previous
    new_object = object_tiles + step_sizes[0].astype(jnp.float32) / 1024.0 * object_direction
    probe_direction = -probe_grad + probe_square / probe_norm_before[0] * probe_previous
    new_probe = probe + step_sizes[1].astype(jnp.float32) / 16384.0 * probe_direction
    return (new_object, object_direction, new_probe, probe_direction)


def solution(mesh):
    return jax.shard_map(
        body,
        mesh=mesh,
        in_specs=(
            P("tile", None, None, None, None),
            P("tile", None, None, None, None),
            P(None, "mode", None, "tile", None),
            P(None, "mode", None, "tile", None),
            P("tile", None, None),
            P(None, "tile"),
            P("tile"),
            P("tile"),
            P(),
            P(),
            P(),
        ),
        out_specs=(
            P("tile", None, None, None, None),
            P("tile", None, None, None, None),
            P(None, "mode", None, "tile", None),
            P(None, "mode", None, "tile", None),
        ),
        check_vma=False,
    )
```

profile of v0, /device:TPU:1, one launch (start us, length us, event | category | flops | bytes accessed | tf_op | source)
XLA Modules:
  0.0 1247.7 jit_solution(10554642321168706119)
XLA Ops:
  7.2 1.5 copy.264
  12.1 11.3 collective-permute-done
  25.1 1.8 fusion.154
  26.9 28.3 %collective-permute-done.1 = bf16[2,2,256,512]{3,2,1,0:T(8,128)(2,1)} collective-permute-done((bf16[2,2,256,512]{3,2,1,0:T(8,128)(2,1)S(1)}, bf16[2,2,256,512]{3,2,1,0:T(8,128)(2,1)}, u32[]{:S(2)}, u32[]{:S(2)}) %collective-permute-start.1) | collective-permute-done | bytes 1048608 | tf_op jit(solution)/shard_map/ppermute | solution.py:16
  55.2 1.4 pad_maximum_fusion
  56.6 6.0 while.1
  57.2 2.4 bitcast_dynamic-update-slice_fusion.2
  60.2 2.4 bitcast_dynamic-update-slice_fusion.2
  62.6 1.4 bitcast_convert_fusion.3
  66.4 200.3 %all-gather.2.cloned.1.call-done = bf16[4,2,2,256,256]{4,0,2,1,3:T(4,128)(2,1)} async-done(((bf16[4,2,2,4,256]{4,0,2,1,3:T(4,128)(2,1)}), bf16[4,2,2,256,256]{4,0,2,1,3:T(4,128)(2,1)}) %all-gather.2.cloned.1.call-update) | async-done | bytes 2097168 | tf_op jit(solution)/shard_map/all_gather | solution.py:100
  266.7 2.3 copy.137
  269.0 1.6 gather_fusion
  270.6 2.0 copy.138
  282.0 1.4 add_convert_fusion.3
  284.7 1.4 fusion.133
  292.4 2.4 add_convert_fusion.2
  298.7 1.7 fusion.125
  304.1 2.1 add_reduce_fusion.1
  311.9 2.1 copy.169
  317.1 82.1 %all-reduce.6.cloned.1.call-done = f32[2,256,256]{1,2,0:T(8,128)} async-done(((f32[2,256,256]{1,2,0:T(8,128)}), f32[2,256,256]{1,2,0:T(8,128)}) %all-reduce.6.cloned.1.call-update) | async-done | bytes 524304 | tf_op jit(solution)/shard_map/psum | solution.py:124
  399.3 1.3 multiply_multiply_fusion
  409.8 2.5 add_reduce_fusion
  421.2 1.4 add_convert_fusion
  423.8 1.5 fusion.109
  431.7 3.0 add_bitcast_fusion
  435.0 2.5 broadcast_in_dim.11
  437.4 11.2 dynamic_update_slice.6
  448.6 1.8 fusion.59
  450.4 12.3 dynamic_update_slice.7
  462.7 3.9 convert_element_type.598
  468.1 1.6 pad_maximum_fusion.1
  469.6 3.1 copy.197
  472.7 6.6 fusion.156
  479.4 50.8 %all-reduce.8.cloned.1.call-done = bf16[2,2,512,512]{2,3,1,0:T(8,128)(2,1)} async-done(((bf16[2,2,512,512]{2,3,1,0:T(8,128)(2,1)}), bf16[2,2,512,512]{2,3,1,0:T(8,128)(2,1)}) %all-reduce.8.cloned.1.call-update) | async-done | bytes 2097168 | tf_op jit(solution)/shard_map/psum | solution.py:154
  530.2 1.4 slice.116
  531.7 3.4 collective-permute-start.2
  535.1 22.3 %collective-permute-done.2 = bf16[2,2,256,512]{2,3,1,0:T(8,128)(2,1)S(1)} collective-permute-done((bf16[2,2,256,512]{2,3,1,0:T(8,128)(2,1)S(1)}, bf16[2,2,256,512]{2,3,1,0:T(8,128)(2,1)S(1)}, u32[]{:S(2)}, u32[]{:S(2)}) %collective-permute-start.2) | collective-permute-done | bytes 1048608 | tf_op jit(solution)/shard_map/ppermute | solution.py:16
  558.4 3.9 collective-permute-start.3
  562.4 1.3 copy.196
  566.9 2.6 copy.195
  570.8 2.8 collective-permute-done.3
  573.6 1.9 multiply_reduce_fusion
  576.2 531.9 %all-reduce.10.cloned.1.call-done = f32[4,2,2,256,256]{4,0,3,2,1:T(4,128)} async-done(((f32[4,2,2,256,256]{4,0,3,2,1:T(4,128)}), f32[4,2,2,256,256]{4,0,3,2,1:T(4,128)}) %all-reduce.10.cloned.1.call-update) | async-done | bytes 4194320
  1108.1 1.5 multiply_reduce_fusion.1
  1109.6 120.8 %all-reduce.1 = (f32[]{:T(128)}, f32[]{:T(128)}) all-reduce(f32[]{:T(128)S(6)} %div.27, f32[]{:T(128)} %multiply_reduce_fusion.1), channel_id=1, replica_groups=mesh['tile'=64,'mode'=4] {'tile','mode'}, use_global_device_ids=true, to_apply=%region_8.9 | all-reduce | flops 2 | bytes 16 | tf_op jit(solution)/shard_map/psum | solution.py:172
  1234.0 2.9 multiply_add_fusion
  1237.0 2.6 copy.200
  1239.6 1.3 copy.201
  (133 shorter events, 65.6 us)
Async XLA Ops:
  7.2 17.8 %copy-start.23 = (s32[2]{0:T(128)S(1)}, s32[2]{0:T(128)}, u32[]{:S(2)}) copy-start(s32[2]{0:T(128)} %param.17) | copy-start | bytes 28
  7.2 259.5 %all-gather.2.cloned.1.call-start = ((), (), s32[]{:S(2)}) async-start(), calls=%async_computation | async-start | bytes 2129920 | tf_op jit(solution)/shard_map/all_gather | solution.py:100
  8.7 390.5 %all-reduce.6.cloned.1.call-start = ((), (), s32[]{:S(2)}) async-start(), calls=%async_computation.1 | async-start | bytes 1048576 | tf_op jit(solution)/shard_map/psum | solution.py:124
  10.1 13.3 %collective-permute-start = (bf16[2,2,256,256]{3,2,1,0:T(8,128)(2,1)S(1)}, bf16[2,2,256,256]{3,2,1,0:T(8,128)(2,1)S(1)}, u32[]{:S(2)}, u32[]{:S(2)}) collective-permute-start(bf16[2,2,256,256]{3,2,1,0:T(8,128)(2,1)S(1)} %convert_bitcast_fusion), channel_id=1, source_target_pairs={{4,0},{8,4},{12,8},{16,12},{20,16},{24,20},{28,24},{32,28},{36,32}... | collective-permute-start | bytes 1572872 | tf_op jit(solution)/shard_map/ppermute | solution.py:16
  23.5 31.7 %collective-permute-start.1 = (bf16[2,2,256,512]{3,2,1,0:T(8,128)(2,1)S(1)}, bf16[2,2,256,512]{3,2,1,0:T(8,128)(2,1)}, u32[]{:S(2)}, u32[]{:S(2)}) collective-permute-start(bf16[2,2,256,512]{3,2,1,0:T(8,128)(2,1)S(1)} %pad_maximum_fusion.3), channel_id=1, source_target_pairs={{32,0},{36,4},{40,8},{44,12},{48,16},{52,20},{56,24},{60,28},{64,3... | collective-permute-start | bytes 3145736 | tf_op jit(solution)/shard_map/ppermute | solution.py:16
  64.2 208.5 %copy-start.2 = (f32[2,256,256]{1,2,0:T(8,128)}, f32[2,256,256]{1,2,0:T(8,128)S(1)}, u32[]{:S(2)}) copy-start(f32[2,256,256]{1,2,0:T(8,128)S(1)} %copy.142) | copy-start | bytes 1572868
  64.4 208.3 %copy-start.4 = (f32[2,256,256]{1,2,0:T(8,128)}, f32[2,256,256]{1,2,0:T(8,128)S(1)}, u32[]{:S(2)}) copy-start(f32[2,256,256]{1,2,0:T(8,128)S(1)} %copy.143) | copy-start | bytes 1572868
  272.8 1.6 copy-start
  279.4 2.5 copy-start.18
  289.9 2.5 copy-start.6
  289.9 2.5 copy-start.8
  304.1 2.2 copy-start.21
  306.3 224.0 %all-reduce.8.cloned.1.call-start = ((), (), s32[]{:S(2)}) async-start(), calls=%async_computation.2 | async-start | bytes 4194304 | tf_op jit(solution)/shard_map/psum | solution.py:154
  408.3 1.3 copy-start.7
  408.3 1.3 copy-start.9
  408.3 1.5 copy-start.11
  418.6 2.5 copy-start.17
  429.1 2.6 copy-start.1
  429.1 2.6 copy-start.3
  429.1 2.6 copy-start.5
  466.5 1.2 copy-start.12
  466.5 1.5 copy-start.13
  466.6 641.5 %all-reduce.10.cloned.1.call-start = ((), (), s32[]{:S(2)}) async-start(), calls=%async_computation.3 | async-start | bytes 8388608
  530.2 27.1 %copy-start.16 = (bf16[2,2,512,512]{2,3,1,0:T(8,128)(2,1)S(1)}, bf16[2,2,512,512]{2,3,1,0:T(8,128)(2,1)}, u32[]{:S(2)}) copy-start(bf16[2,2,512,512]{2,3,1,0:T(8,128)(2,1)} %all-reduce.8.cloned.1.call-done) | copy-start | bytes 6291460
  531.7 30.7 %copy-start.10 = (f32[1,2,2,256,256]{4,3,2,1,0:T(8,128)S(1)}, f32[1,2,2,256,256]{4,3,2,1,0:T(8,128)}, u32[]{:S(2)}) copy-start(f32[1,2,2,256,256]{4,3,2,1,0:T(8,128)} %param.11) | copy-start | bytes 3145732
  531.7 25.6 %collective-permute-start.2 = (bf16[2,2,256,512]{2,3,1,0:T(8,128)(2,1)S(1)}, bf16[2,2,256,512]{2,3,1,0:T(8,128)(2,1)S(1)}, u32[]{:S(2)}, u32[]{:S(2)}) collective-permute-start(bf16[2,2,256,512]{2,3,1,0:T(8,128)(2,1)S(1)} %slice.116), channel_id=1, source_target_pairs={{0,32},{4,36},{8,40},{12,44},{16,48},{20,52},{24,56},{28,60},{32,6... | collective-permute-start | bytes 3145736 | tf_op jit(solution)/shard_map/ppermute | solution.py:16
  557.5 6.8 copy-start.22
  558.4 15.2 %collective-permute-start.3 = (bf16[2,2,256,256]{2,3,1,0:T(8,128)(2,1)}, bf16[2,2,256,256]{2,3,1,0:T(8,128)(2,1)}, u32[]{:S(2)}, u32[]{:S(2)}) collective-permute-start(bf16[2,2,256,256]{2,3,1,0:T(8,128)(2,1)} %slice.159), channel_id=1, source_target_pairs={{0,4},{4,8},{8,12},{12,16},{16,20},{20,24},{24,28},{28,32},{32,36}... | collective-permute-start | bytes 1572872 | tf_op jit(solution)/shard_map/ppermute | solution.py:16
  562.4 7.2 copy-start.24
  563.7 667.4 %copy-start.19 = (f32[4,2,2,4,256]{4,3,2,1,0:T(4,128)S(1)}, f32[4,2,2,4,256]{4,3,2,1,0:T(4,128)}, u32[]{:S(2)}) copy-start(f32[4,2,2,4,256]{4,3,2,1,0:T(4,128)} %param.13) | copy-start | bytes 196612
  563.7 667.4 %copy-start.20 = (f32[4,2,2,4,256]{4,3,2,1,0:T(4,128)S(1)}, f32[4,2,2,4,256]{4,3,2,1,0:T(4,128)}, u32[]{:S(2)}) copy-start(f32[4,2,2,4,256]{4,3,2,1,0:T(4,128)} %param.14) | copy-start | bytes 196612
  566.9 667.1 %copy-start.14 = (f32[1,2,2,256,256]{3,4,2,1,0:T(8,128)S(1)}, f32[1,2,2,256,256]{3,4,2,1,0:T(8,128)}, u32[]{:S(2)}) copy-start(f32[1,2,2,256,256]{3,4,2,1,0:T(8,128)} %copy.196) | copy-start | bytes 3145732
  1237.0 2.6 copy-start.15
Sparse Core Ops, SparseCore 0:
  10.3 256.2 all-gather.1
  306.4 92.8 all-reduce.5
  466.7 63.5 all-reduce.7
  532.7 575.3 all-reduce.9
where the time goes:
time: 1250 us
  waiting for transfers between devices  930 us (74%)
  blocking collectives  121 us (10%)
  matrix products  73.2 us (6%)
  local copies, waits for them, and re-layouts  62.1 us (5%)
  between operations  28.2 us (2%)
  other arithmetic  23.5 us (2%)
    unnamed x5, waiting for transfers between devices  532 us
    all_gather x1, waiting for transfers between devices, body(): lax.all_gather(probe.astype(jnp.bfloat16), 'tile', axis=3, tiled=True)  200 us
    psum x1, blocking collectives, body(): lax.psum((object_sum, probe_sum), ('tile', 'mode'))  121 us
    psum x1, waiting for transfers between devices, body(): power = lax.psum(partial_power, 'mode')  82.1 us
    ppermute x4, waiting for transfers between devices, from_behind(): return lax.ppermute(block, axis, route)  64.6 us
    psum x1, waiting for transfers between devices, body(): lax.psum(region_grad.astype(jnp.bfloat16), 'mode').astype(jnp.float32)  50.8 us
    dot_general x24, matrix products, left_product(): jnp.einsum('ij,...jl->...il', table, right_data, preferred_element_type=j...  35.8 us
    dot_general x24, matrix products, right_product(): jnp.einsum('...jk,kl->...jl', left_data, table, preferred_element_type=jn...  30.7 us
  transfers between devices with their start and end apart: 8, of which 8 were waited for; matrix products, arithmetic and copies ran while one was open for 3% of the time, Pallas kernels for 0%

commit v1 on v0

--- a/solution.py
+++ b/solution.py
@@ -1,3 +1,4 @@
+import functools
 import math
 import jax
 import jax.numpy as jnp
@@ -8,6 +9,13 @@
 MODES = 8
 SCAN_COUNT = 4
 residual_weight = 2.0
+
+
+def connect_the_tasks(q_in, dev_axis, which_axis):
+    return jax.lax.psum(jax.lax.psum(q_in, axis_name=dev_axis), axis_name=which_axis)
+
+
+_step_on_knots = functools.partial(connect_the_tasks, dev_axis="tile", which_axis="mode")
 
 
 def from_behind(block, axis, distance):
@@ -169,7 +177,7 @@
     probe_grad = lax.psum_scatter(probe_local, "tile", scatter_dimension=3, tiled=True)
     object_sum = jnp.sum(tile_grad * tile_grad) / float(mode_count)
     probe_sum = jnp.sum(probe_grad * probe_grad)
-    object_total, probe_total = lax.psum((object_sum, probe_sum), ("tile", "mode"))
+    object_total, probe_total = _step_on_knots((object_sum, probe_sum))
     object_square = object_total / float(tile_count * layers * 2 * tile_side * tile_side)
     probe_square = probe_total / float(SCAN_COUNT * MODES * 2 * width * width)
     object_direction = -tile_grad[None] + object_square / object_norm_before[0] * object_previous

time: 1250 us -> 1340 us (1.072)
  blocking collectives: 121 us -> 212 us
    psum x1 -> x2, blocking collectives: 121 us -> 212 us  [the longest x1 131 us: connect_the_tasks(): jax.lax.psum(q_in, axis_name=dev_axis)]
where the time goes in v1:
time: 1340 us
  waiting for transfers between devices  929 us (69%)
  blocking collectives  212 us (16%)
  matrix products  73.2 us (5%)
  local copies, waits for them, and re-layouts  62.4 us (5%)
  between operations  28.2 us (2%)
  other arithmetic  23.6 us (2%)
    unnamed x5, waiting for transfers between devices  532 us
    all_gather x1, waiting for transfers between devices, body(): lax.all_gather(probe.astype(jnp.bfloat16), 'tile', axis=3, tiled=True)  200 us
    psum x1, blocking collectives, connect_the_tasks(): jax.lax.psum(q_in, axis_name=dev_axis)  131 us
    psum x1, waiting for transfers between devices, body(): power = lax.psum(partial_power, 'mode')  81.9 us
    psum x1, blocking collectives, connect_the_tasks(): jax.lax.psum(jax.lax.psum(q_in, axis_name=dev_axis), axis_name=which_axis)  81.2 us
    ppermute x4, waiting for transfers between devices, from_behind(): return lax.ppermute(block, axis, route)  64.6 us
    psum x1, waiting for transfers between devices, body(): lax.psum(region_grad.astype(jnp.bfloat16), 'mode').astype(jnp.float32)  50.8 us
    dot_general x24, matrix products, left_product(): jnp.einsum('ij,...jl->...il', table, right_data, preferred_element_type=j...  35.8 us
  transfers between devices with their start and end apart: 8, of which 8 were waited for; matrix products, arithmetic and copies ran while one was open for 3% of the time, Pallas kernels for 0%

profile of v1, /device:TPU:1, one launch (start us, length us, event | category | flops | bytes accessed | tf_op | source)
XLA Modules:
  0.0 1338.3 jit_solution(5678504297354861399)
XLA Ops:
  7.2 1.5 copy.264
  12.1 11.3 collective-permute-done
  25.1 1.8 fusion.154
  27.0 28.2 %collective-permute-done.1 = bf16[2,2,256,512]{3,2,1,0:T(8,128)(2,1)} collective-permute-done((bf16[2,2,256,512]{3,2,1,0:T(8,128)(2,1)S(1)}, bf16[2,2,256,512]{3,2,1,0:T(8,128)(2,1)}, u32[]{:S(2)}, u32[]{:S(2)}) %collective-permute-start.1) | collective-permute-done | bytes 1048608 | tf_op jit(solution)/shard_map/ppermute | solution.py:24
  55.2 1.4 pad_maximum_fusion
  56.6 6.3 while.1
  57.3 2.4 bitcast_dynamic-update-slice_fusion.2
  60.4 2.4 bitcast_dynamic-update-slice_fusion.2
  62.8 1.4 bitcast_convert_fusion.3
  66.7 200.1 %all-gather.2.cloned.1.call-done = bf16[4,2,2,256,256]{4,0,2,1,3:T(4,128)(2,1)} async-done(((bf16[4,2,2,4,256]{4,0,2,1,3:T(4,128)(2,1)}), bf16[4,2,2,256,256]{4,0,2,1,3:T(4,128)(2,1)}) %all-gather.2.cloned.1.call-update) | async-done | bytes 2097168 | tf_op jit(solution)/shard_map/all_gather | solution.py:108
  266.8 2.3 copy.137
  269.1 1.6 gather_fusion
  270.7 2.0 copy.138
  282.1 1.4 add_convert_fusion.3
  284.8 1.4 fusion.133
  292.5 2.4 add_convert_fusion.2
  298.8 1.7 fusion.125
  304.2 2.1 add_reduce_fusion.1
  312.1 2.0 copy.169
  317.3 81.9 %all-reduce.7.cloned.1.call-done = f32[2,256,256]{1,2,0:T(8,128)} async-done(((f32[2,256,256]{1,2,0:T(8,128)}), f32[2,256,256]{1,2,0:T(8,128)}) %all-reduce.7.cloned.1.call-update) | async-done | bytes 524304 | tf_op jit(solution)/shard_map/psum | solution.py:132
  399.2 1.3 multiply_multiply_fusion
  409.8 2.5 add_reduce_fusion
  421.1 1.4 add_convert_fusion
  423.8 1.5 fusion.109
  431.6 3.0 add_bitcast_fusion
  434.9 2.5 broadcast_in_dim.11
  437.4 11.2 dynamic_update_slice.6
  448.6 1.8 fusion.59
  450.4 12.3 dynamic_update_slice.7
  462.7 3.8 convert_element_type.598
  468.1 1.6 pad_maximum_fusion.1
  469.6 3.1 copy.197
  472.7 6.6 fusion.156
  479.4 50.8 %all-reduce.9.cloned.1.call-done = bf16[2,2,512,512]{2,3,1,0:T(8,128)(2,1)} async-done(((bf16[2,2,512,512]{2,3,1,0:T(8,128)(2,1)}), bf16[2,2,512,512]{2,3,1,0:T(8,128)(2,1)}) %all-reduce.9.cloned.1.call-update) | async-done | bytes 2097168 | tf_op jit(solution)/shard_map/psum | solution.py:162
  530.2 1.4 slice.116
  531.7 3.4 collective-permute-start.2
  535.0 22.3 %collective-permute-done.2 = bf16[2,2,256,512]{2,3,1,0:T(8,128)(2,1)S(1)} collective-permute-done((bf16[2,2,256,512]{2,3,1,0:T(8,128)(2,1)S(1)}, bf16[2,2,256,512]{2,3,1,0:T(8,128)(2,1)S(1)}, u32[]{:S(2)}, u32[]{:S(2)}) %collective-permute-start.2) | collective-permute-done | bytes 1048608 | tf_op jit(solution)/shard_map/ppermute | solution.py:24
  558.4 4.0 collective-permute-start.3
  562.3 1.3 copy.196
  566.9 2.6 copy.195
  570.8 2.8 collective-permute-done.3
  573.6 1.9 multiply_reduce_fusion
  576.2 531.6 %all-reduce.11.cloned.1.call-done = f32[4,2,2,256,256]{4,0,3,2,1:T(4,128)} async-done(((f32[4,2,2,256,256]{4,0,3,2,1:T(4,128)}), f32[4,2,2,256,256]{4,0,3,2,1:T(4,128)}) %all-reduce.11.cloned.1.call-update) | async-done | bytes 4194320
  1107.8 1.5 multiply_reduce_fusion.1
  1109.3 130.5 %all-reduce.1 = (f32[]{:T(128)}, f32[]{:T(128)}) all-reduce(f32[]{:T(128)S(6)} %div.27, f32[]{:T(128)} %multiply_reduce_fusion.1), channel_id=1, replica_groups=mesh['tile'=64,'mode'=4] {'tile'}, use_global_device_ids=true, to_apply=%region_8.9 | all-reduce | flops 2 | bytes 16 | tf_op jit(solution)/shard_map/psum | solution.py:15
  1239.8 81.2 %all-reduce.2 = (f32[]{:T(128)}, f32[]{:T(128)}) all-reduce(f32[]{:T(128)} %get-tuple-element.36, f32[]{:T(128)} %get-tuple-element.37), channel_id=1, replica_groups=mesh['tile'=64,'mode'=4] {'mode'}, use_global_device_ids=true, to_apply=%region_9.10 | all-reduce | flops 2 | bytes 16 | tf_op jit(solution)/shard_map/psum | solution.py:15
  1324.6 2.9 multiply_add_fusion
  1327.5 2.6 copy.200
  (134 shorter events, 67.0 us)
Async XLA Ops:
  7.2 17.8 %copy-start.23 = (s32[2]{0:T(128)S(1)}, s32[2]{0:T(128)}, u32[]{:S(2)}) copy-start(s32[2]{0:T(128)} %param.17) | copy-start | bytes 28
  7.2 259.6 %all-gather.2.cloned.1.call-start = ((), (), s32[]{:S(2)}) async-start(), calls=%async_computation | async-start | bytes 2129920 | tf_op jit(solution)/shard_map/all_gather | solution.py:108
  8.7 390.5 %all-reduce.7.cloned.1.call-start = ((), (), s32[]{:S(2)}) async-start(), calls=%async_computation.1 | async-start | bytes 1048576 | tf_op jit(solution)/shard_map/psum | solution.py:132
  10.1 13.3 collective-permute-start
  23.5 31.7 %collective-permute-start.1 = (bf16[2,2,256,512]{3,2,1,0:T(8,128)(2,1)S(1)}, bf16[2,2,256,512]{3,2,1,0:T(8,128)(2,1)}, u32[]{:S(2)}, u32[]{:S(2)}) collective-permute-start(bf16[2,2,256,512]{3,2,1,0:T(8,128)(2,1)S(1)} %pad_maximum_fusion.3), channel_id=1, source_target_pairs={{32,0},{36,4},{40,8},{44,12},{48,16},{52,20},{56,24},{60,28},{64,3... | collective-permute-start | bytes 3145736 | tf_op jit(solution)/shard_map/ppermute | solution.py:24
  64.4 208.4 %copy-start.2 = (f32[2,256,256]{1,2,0:T(8,128)}, f32[2,256,256]{1,2,0:T(8,128)S(1)}, u32[]{:S(2)}) copy-start(f32[2,256,256]{1,2,0:T(8,128)S(1)} %copy.142) | copy-start | bytes 1572868
  64.6 208.2 %copy-start.4 = (f32[2,256,256]{1,2,0:T(8,128)}, f32[2,256,256]{1,2,0:T(8,128)S(1)}, u32[]{:S(2)}) copy-start(f32[2,256,256]{1,2,0:T(8,128)S(1)} %copy.143) | copy-start | bytes 1572868
  272.9 1.6 copy-start
  279.5 2.5 copy-start.18
  290.0 2.5 copy-start.6
  290.0 2.5 copy-start.8
  304.2 2.2 copy-start.21
  306.4 223.8 %all-reduce.9.cloned.1.call-start = ((), (), s32[]{:S(2)}) async-start(), calls=%async_computation.2 | async-start | bytes 4194304 | tf_op jit(solution)/shard_map/psum | solution.py:162
  408.2 1.3 copy-start.7
  408.3 1.3 copy-start.9
  408.3 1.5 copy-start.11
  418.6 2.5 copy-start.17
  429.1 2.6 copy-start.1
  429.1 2.6 copy-start.3
  429.1 2.6 copy-start.5
  466.5 1.2 copy-start.12
  466.5 1.5 copy-start.13
  466.5 641.2 %all-reduce.11.cloned.1.call-start = ((), (), s32[]{:S(2)}) async-start(), calls=%async_computation.3 | async-start | bytes 8388608
  530.2 27.1 %copy-start.16 = (bf16[2,2,512,512]{2,3,1,0:T(8,128)(2,1)S(1)}, bf16[2,2,512,512]{2,3,1,0:T(8,128)(2,1)}, u32[]{:S(2)}) copy-start(bf16[2,2,512,512]{2,3,1,0:T(8,128)(2,1)} %all-reduce.9.cloned.1.call-done) | copy-start | bytes 6291460
  531.6 30.7 %copy-start.10 = (f32[1,2,2,256,256]{4,3,2,1,0:T(8,128)S(1)}, f32[1,2,2,256,256]{4,3,2,1,0:T(8,128)}, u32[]{:S(2)}) copy-start(f32[1,2,2,256,256]{4,3,2,1,0:T(8,128)} %param.11) | copy-start | bytes 3145732
  531.7 25.6 %collective-permute-start.2 = (bf16[2,2,256,512]{2,3,1,0:T(8,128)(2,1)S(1)}, bf16[2,2,256,512]{2,3,1,0:T(8,128)(2,1)S(1)}, u32[]{:S(2)}, u32[]{:S(2)}) collective-permute-start(bf16[2,2,256,512]{2,3,1,0:T(8,128)(2,1)S(1)} %slice.116), channel_id=1, source_target_pairs={{0,32},{4,36},{8,40},{12,44},{16,48},{20,52},{24,56},{28,60},{32,6... | collective-permute-start | bytes 3145736 | tf_op jit(solution)/shard_map/ppermute | solution.py:24
  557.5 6.8 copy-start.22
  558.4 15.2 %collective-permute-start.3 = (bf16[2,2,256,256]{2,3,1,0:T(8,128)(2,1)}, bf16[2,2,256,256]{2,3,1,0:T(8,128)(2,1)}, u32[]{:S(2)}, u32[]{:S(2)}) collective-permute-start(bf16[2,2,256,256]{2,3,1,0:T(8,128)(2,1)} %slice.159), channel_id=1, source_target_pairs={{0,4},{4,8},{8,12},{12,16},{16,20},{20,24},{24,28},{28,32},{32,36}... | collective-permute-start | bytes 1572872 | tf_op jit(solution)/shard_map/ppermute | solution.py:24
  562.3 7.2 copy-start.24
  563.6 758.1 %copy-start.19 = (f32[4,2,2,4,256]{4,3,2,1,0:T(4,128)S(1)}, f32[4,2,2,4,256]{4,3,2,1,0:T(4,128)}, u32[]{:S(2)}) copy-start(f32[4,2,2,4,256]{4,3,2,1,0:T(4,128)} %param.13) | copy-start | bytes 196612
  563.6 758.1 %copy-start.20 = (f32[4,2,2,4,256]{4,3,2,1,0:T(4,128)S(1)}, f32[4,2,2,4,256]{4,3,2,1,0:T(4,128)}, u32[]{:S(2)}) copy-start(f32[4,2,2,4,256]{4,3,2,1,0:T(4,128)} %param.14) | copy-start | bytes 196612
  566.9 757.7 %copy-start.14 = (f32[1,2,2,256,256]{3,4,2,1,0:T(8,128)S(1)}, f32[1,2,2,256,256]{3,4,2,1,0:T(8,128)}, u32[]{:S(2)}) copy-start(f32[1,2,2,256,256]{3,4,2,1,0:T(8,128)} %copy.196) | copy-start | bytes 3145732
  1327.5 2.6 copy-start.15
Sparse Core Ops, SparseCore 0:
  10.3 256.3 all-gather.1
  306.5 92.7 all-reduce.6
  466.7 63.4 all-reduce.8
  532.7 575.0 all-reduce.10
